TPU v7x, 32 devices: a whole 2x2x4 slice. The times are simulated.
32 devices in a mesh: mem: 4 (over x, core), band: 8 (over z, y).
Axes of the slice: x: 2, y: 2, z: 4, core: 2. Of those that a mesh axis runs over, the one named last changes fastest.
Arguments:
- sample_collection: float32 [24, 3, 64, 4096], P('mem', None, 'band'), may hold values from -6 to 6
- seabed_profile: float32 [64, 4096], P('band'), may hold values from 0.5 to 2
- gauge_grid_position: int32 [32, 128], P('band'), may hold values from 0 to 262143, as said below
- observed_values: float32 [32, 128], P('band'), may hold values from -6 to 6
- error_scale: float32 [32, 128], P('band'), may hold values from 0.3 to 3
- perturbation: float32 [24, 32, 128], P('mem', 'band'), may hold values from -6 to 6
- inflation: float32 [1], replicated, may hold values from 1 to 16
Outputs:
- analysis: float32 [24, 3, 64, 4096], P('mem', None, 'band')
Inputs may be any that keep to these rules, and one draw needn't show every extreme that they name: Every entry in row r of gauge_grid_position lies in grid rows b * 8 to (b + 1) * 8 - 1 with b = r // 4; cells may repeat.
All inputs are finite; a program needn't handle non-finite values.
Results may differ from a plain program's by a relative error of at most 0.000071.
Values sent between devices are 32-bit elements; how exact they have to be, the bound alone decides.
No kernel may reach another device: no remote copies, remote signals or barrier semaphores. Data moves between devices by JAX's collectives and lax.ppermute only.
A program may use at most 128 MiB of HBM per device.

v0:
```python
import math
import jax
import jax.numpy as jnp
from jax import lax
from jax.sharding import PartitionSpec as P

STEPS = 2
courant = 0.5
coriolis_base = 0.15
coriolis_slope = 0.3


def with_halo(cells, sides, width):
    for axis, dim in sides:
        count = lax.axis_size(axis)
        ends = count - 1
        head = lax.slice_in_dim(cells, 0, width, axis=dim)
        tail = lax.slice_in_dim(cells, cells.shape[dim] - width, cells.shape[dim], axis=dim)
        cells = jnp.concatenate(
            [
                lax.ppermute(tail, axis, [(i, (i + 1) % count) for i in range(ends)]),
                cells,
                lax.ppermute(head, axis, [((i + 1) % count, i) for i in range(ends)]),
            ],
            axis=dim,
        )
    return cells


def east_diff(quantity):
    return (jnp.roll(quantity, -1, axis=-1) - jnp.roll(quantity, 1, axis=-1)) * 0.5


def body(
    sample_collection,
    seabed_profile,
    gauge_grid_position,
    observed_values,
    error_scale,
    perturbation,
    inflation,
):
    local_members, _, band_rows, columns = sample_collection.shape
    total_rows = band_rows * lax.axis_size("band")
    sample_trajectories = local_members * lax.axis_size("mem")
    first_row = lax.axis_index("band") * band_rows
    global_rows = (first_row + jnp.arange(band_rows)).astype(jnp.float32)
    earth_spin_turning = (coriolis_base + coriolis_slope * (global_rows + 0.5) / total_rows)[
        :, None
    ]
    surface_height, eastward_velocity_field, northward_velocity_field = (
        sample_collection[:, 0],
        sample_collection[:, 1],
        sample_collection[:, 2],
    )
    for _ in range(STEPS):
        rim_flux = with_halo(seabed_profile * northward_velocity_field, (("band", 1),), 1)
        surface_height = surface_height - courant * (
            east_diff(seabed_profile * eastward_velocity_field)
            + (rim_flux[:, 2:] - rim_flux[:, :-2]) * 0.5
        )
        eastward_velocity_field = (
            eastward_velocity_field
            - courant * east_diff(surface_height)
            + earth_spin_turning * northward_velocity_field
        )
        rim_height = with_halo(surface_height, (("band", 1),), 1)
        northward_velocity_field = (
            northward_velocity_field
            - courant * ((rim_height[:, 2:] - rim_height[:, :-2]) * 0.5)
            - earth_spin_turning * eastward_velocity_field
        )
    prior_model_outputs = jnp.stack(
        [surface_height, eastward_velocity_field, northward_velocity_field], axis=1
    )
    local_cells = gauge_grid_position.reshape(-1) - first_row * columns
    modelled_water_levels = jnp.take(surface_height.reshape(local_members, -1), local_cells, axis=1)
    obs_scale = error_scale.reshape(-1)
    factor = inflation[0]
    innovation = (
        observed_values.reshape(-1)
        + jnp.sqrt(factor) * obs_scale * perturbation.reshape(local_members, -1)
        - modelled_water_levels
    ) / obs_scale
    norm_factor = math.sqrt(sample_trajectories - 1)
    centre = lax.psum(jnp.sum(modelled_water_levels, axis=0), "mem") / sample_trajectories
    spread_local = (modelled_water_levels - centre) / (obs_scale * norm_factor)
    spread, innovation_all = (
        lax.all_gather(spread_local, "mem", axis=0, tiled=True),
        lax.all_gather(innovation, "mem", axis=0, tiled=True),
    )
    gram_local = jnp.dot(
        spread, spread.T, precision=lax.Precision.HIGHEST, preferred_element_type=jnp.float32
    )
    cross_local = jnp.dot(
        spread,
        innovation_all.T,
        precision=lax.Precision.HIGHEST,
        preferred_element_type=jnp.float32,
    )
    gram_matrix, cross_term = lax.psum((gram_local, cross_local), "band")
    system = gram_matrix + factor * jnp.eye(sample_trajectories, dtype=jnp.float32)
    cholesky_lower = jnp.linalg.cholesky(system)
    middle = lax.linalg.triangular_solve(cholesky_lower, cross_term, left_side=True, lower=True)
    weights = lax.linalg.triangular_solve(
        cholesky_lower, middle, left_side=True, lower=True, transpose_a=True
    )
    assimilate_update_step = (
        jnp.eye(sample_trajectories, dtype=jnp.float32)
        + (weights - jnp.mean(weights, axis=0, keepdims=True)) / norm_factor
    )
    own_rows = lax.dynamic_slice_in_dim(
        assimilate_update_step, lax.axis_index("mem") * local_members, local_members, 0
    )
    return lax.psum_scatter(
        jnp.tensordot(
            own_rows, prior_model_outputs, axes=([0], [0]), precision=lax.Precision.HIGHEST
        ),
        "mem",
        scatter_dimension=0,
        tiled=True,
    )


def solution(mesh):
    in_specs = (
        P("mem", None, "band", None),
        P("band", None),
        P("band", None),
        P("band", None),
        P("band", None),
        P("mem", "band", None),
        P(),
    )
    out_specs = P("mem", None, "band", None)
    return jax.shard_map(body, mesh=mesh, in_specs=in_specs, out_specs=out_specs, check_vma=False)
```

profile of v0, /device:TPU:0, one launch (start us, length us, event | category | flops | bytes accessed | tf_op | source)
XLA Modules:
  0.0 242.2 jit_solution(15384957077126619160)
XLA Ops:
  6.5 2.7 %fusion.57 = (f32[6,1,8,4096]{3,2,1,0:T(8,128)}, f32[6,1,8,4096]{3,2,1,0:T(8,128)S(1)}, f32[6,1,8,4096]{3,2,1,0:T(8,128)S(1)}) fusion(f32[6,3,8,4096]{3,2,1,0:T(8,128)} %param.7), kind=kLoop, calls=%fused_computation.92 | loop fusion | bytes 4718592 | tf_op jit(solution)/shard_map/slice | solution.py:52
  11.6 5.5 %collective-permute-start.1 = (f32[6,1,4096]{2,0,1:T(8,128)S(1)}, f32[6,1,4096]{2,0,1:T(8,128)S(1)}, u32[]{:S(2)}, u32[]{:S(2)}) collective-permute-start(f32[6,1,4096]{2,0,1:T(8,128)S(1)} %get-tuple-element.41), channel_id=1, source_target_pairs={{0,1},{1,2},{2,3},{3,4},{4,5},{5,6},{6,7},{8,9},{9,10},{10,11},{11... | collective-permute-start | bytes 294920 | tf_op jit(solution)/shard_map/ppermute | solution.py:21
  17.1 1.7 fusion.68
  21.7 2.6 %fusion.22 = f32[6,8,4096]{2,0,1:T(8,128)S(1)} fusion(f32[6,8,4096]{2,0,1:T(8,128)S(1)} %get-tuple-element.45, f32[6,1,4096]{2,0,1:T(8,128)S(1)} %collective-permute-done.1, f32[6,1,4096]{2,0,1:T(8,128)S(1)} %collective-permute-done, f32[6,8,1]{2,0,1:T(8,128)S(1)} %get-tuple-element.37, f32[6,8,4095]{2,0,1:T(8,128)} %get-tuple-element.39, ...), kind=kLoop, calls=%fused_computation.30 | loop fusion | flops 1769472 | bytes 4128768 | tf_op jit(solution)/shard_map/sub | solution.py:58
  26.0 5.0 %collective-permute-start.3 = (f32[6,1,4096]{2,0,1:T(8,128)S(1)}, f32[6,1,4096]{2,0,1:T(8,128)S(1)}, u32[]{:S(2)}, u32[]{:S(2)}) collective-permute-start(f32[6,1,4096]{2,0,1:T(8,128)S(1)} %get-tuple-element.31), channel_id=1, source_target_pairs={{0,1},{1,2},{2,3},{3,4},{4,5},{5,6},{6,7},{8,9},{9,10},{10,11},{11... | collective-permute-start | bytes 294920 | tf_op jit(solution)/shard_map/ppermute | solution.py:21
  32.8 3.0 %collective-permute-done.3 = f32[6,1,4096]{2,0,1:T(8,128)S(1)} collective-permute-done((f32[6,1,4096]{2,0,1:T(8,128)S(1)}, f32[6,1,4096]{2,0,1:T(8,128)S(1)}, u32[]{:S(2)}, u32[]{:S(2)}) %collective-permute-start.3) | collective-permute-done | bytes 98336 | tf_op jit(solution)/shard_map/ppermute | solution.py:21
  37.8 5.0 %collective-permute-start.5 = (f32[6,1,4096]{2,0,1:T(8,128)S(1)}, f32[6,1,4096]{2,0,1:T(8,128)S(1)}, u32[]{:S(2)}, u32[]{:S(2)}) collective-permute-start(f32[6,1,4096]{2,0,1:T(8,128)S(1)} %get-tuple-element.29), channel_id=1, source_target_pairs={{0,1},{1,2},{2,3},{3,4},{4,5},{5,6},{6,7},{8,9},{9,10},{10,11},{11... | collective-permute-start | bytes 294920 | tf_op jit(solution)/shard_map/ppermute | solution.py:21
  42.9 1.7 collective-permute-done.4
  44.6 3.0 %collective-permute-done.5 = f32[6,1,4096]{2,0,1:T(8,128)S(1)} collective-permute-done((f32[6,1,4096]{2,0,1:T(8,128)S(1)}, f32[6,1,4096]{2,0,1:T(8,128)S(1)}, u32[]{:S(2)}, u32[]{:S(2)}) %collective-permute-start.5) | collective-permute-done | bytes 98336 | tf_op jit(solution)/shard_map/ppermute | solution.py:21
  48.0 1.6 fusion.58
  50.5 9.0 %copy.26 = f32[6,32768]{0,1:T(8,128)} copy(f32[6,32768]{1,0:T(8,128)S(1)} %bitcast.84) | data formatting | bytes 1572864 | tf_op jit(solution)/shard_map/reshape | solution.py:77
  59.5 6.8 %gather_fusion = f32[512,6]{1,0:T(8,128)S(1)} fusion(f32[6,32768]{0,1:T(8,128)} %copy.26, s32[1024]{0:T(1024)S(1)} %pad_clamp_fusion), kind=kCustom, calls=%fused_computation | custom fusion | bytes 26624 | tf_op jit(solution)/shard_map/jit(_take)/gather | solution.py:77
  66.5 6.9 %psum.21 = f32[512]{0:T(512)S(1)} all-reduce(f32[512]{0:T(512)S(1)} %select_reduce_fusion), channel_id=1, replica_groups=mesh['mem'=4,'band'=8] {'mem'}, use_global_device_ids=true, to_apply=%region_1.2 | all-reduce | flops 512 | bytes 4096 | tf_op jit(solution)/shard_map/psum | solution.py:86
  73.4 2.2 fusion.34
  76.7 5.2 %all-gather = f32[4,6,512]{2,1,0:T(8,128)S(1)} all-gather(f32[1,6,512]{2,1,0:T(8,128)S(1)} %copy.27), channel_id=1, replica_groups=mesh['mem'=4,'band'=8] {'mem'}, dimensions={0}, use_global_device_ids=true | all-gather | bytes 61440 | tf_op jit(solution)/shard_map/all_gather | solution.py:89
  83.0 5.2 %all-gather.1 = f32[4,6,512]{2,1,0:T(8,128)S(1)} all-gather(f32[1,6,512]{2,1,0:T(8,128)S(1)} %copy.30), channel_id=1, replica_groups=mesh['mem'=4,'band'=8] {'mem'}, dimensions={0}, use_global_device_ids=true | all-gather | bytes 61440 | tf_op jit(solution)/shard_map/all_gather | solution.py:90
  88.6 35.7 %all-reduce = (f32[24,24]{1,0:T(8,128)S(1)}, f32[24,24]{1,0:T(8,128)S(1)}) all-reduce(f32[24,24]{1,0:T(8,128)S(1)} %fusion.72, f32[24,24]{1,0:T(8,128)S(1)} %fusion.71), channel_id=1, replica_groups=mesh['mem'=4,'band'=8] {'band'}, use_global_device_ids=true, to_apply=%region_5.6 | all-reduce | flops 1152 | bytes 9216 | tf_op jit(solution)/shard_map/psum | solution.py:101
  124.3 2.2 cholesky.13
  127.7 1.8 custom-call.8
  131.3 4.7 %collective-permute-start.7 = (f32[6,1,4096]{2,0,1:T(8,128)}, f32[6,1,4096]{2,0,1:T(8,128)S(1)}, u32[]{:S(2)}, u32[]{:S(2)}) collective-permute-start(f32[6,1,4096]{2,0,1:T(8,128)} %get-tuple-element.23), channel_id=1, source_target_pairs={{0,1},{1,2},{2,3},{3,4},{4,5},{5,6},{6,7},{8,9},{9,10},{10,11},{11... | collective-permute-start | bytes 294920 | tf_op jit(solution)/shard_map/ppermute | solution.py:21
  138.6 2.1 fusion.10
  140.8 8.1 %fusion = f32[24,3,8,4096]{3,0,2,1:T(8,128)S(1)} fusion(f32[6,1,8,4096]{3,0,2,1:T(8,128)S(1)} %get-tuple-element.9, f32[6,1,8,4096]{3,0,2,1:T(8,128)S(1)} %bitcast.86, f32[6,1,8,4096]{3,0,2,1:T(8,128)S(1)} %bitcast.85, f32[24,24]{1,0:T(8,128)S(1)} %get-tuple-element.49, s32[]{:T(128)S(6)} %select_n.31, pred[24,24]{1,0:T(8,128)(4,1)S(1)} %iota_compare_fusion.1, ...), kind=kOutput, calls=%fused_computation.1 | convolution fusion | flops 171049536 | bytes 12588548 | tf_op jit(solution)/shard_map/dot_general | solution.py:116
  148.8 9.1 %copy.31 = f32[24,3,8,4096]{3,2,1,0:T(8,128)} copy(f32[24,3,8,4096]{3,0,2,1:T(8,128)S(1)} %fusion) | data formatting | bytes 18874368 | tf_op jit(solution)/shard_map/dot_general | solution.py:116
  158.0 77.3 %reduce-scatter.2.cloned.1.call-done = f32[6,3,8,4096]{3,2,1,0:T(8,128)} async-done(((f32[24,3,8,4096]{3,2,1,0:T(8,128)}), f32[6,3,8,4096]{3,2,1,0:T(8,128)}) %reduce-scatter.2.cloned.1.call-update) | async-done | bytes 2359312 | tf_op jit(solution)/shard_map/reduce_scatter | solution.py:115
  (59 shorter events, 19.6 us)
Async XLA Ops:
  6.5 2.8 %copy-start = (f32[8,4096]{1,0:T(8,128)S(1)}, f32[8,4096]{1,0:T(8,128)}, u32[]{:S(2)}) copy-start(f32[8,4096]{1,0:T(8,128)} %param.8) | copy-start | bytes 393220
  6.5 228.8 %reduce-scatter.2.cloned.1.call-start = ((), (), s32[]{:S(2)}) async-start(), calls=%async_computation.1 | async-start | bytes 11796480 | tf_op jit(solution)/shard_map/reduce_scatter | solution.py:115
  10.2 8.7 %copy-start.4 = (s32[4,128]{1,0:T(4,128)S(1)}, s32[4,128]{1,0:T(4,128)}, u32[]{:S(2)}) copy-start(s32[4,128]{1,0:T(4,128)} %param.9) | copy-start | bytes 6148
  10.3 9.4 %copy-start.1 = (f32[6,4,128]{2,1,0:T(4,128)S(1)}, f32[6,4,128]{2,1,0:T(4,128)}, u32[]{:S(2)}) copy-start(f32[6,4,128]{2,1,0:T(4,128)} %param.12) | copy-start | bytes 36868
  10.3 10.3 %copy-start.2 = (f32[4,128]{1,0:T(4,128)S(1)}, f32[4,128]{1,0:T(4,128)}, u32[]{:S(2)}) copy-start(f32[4,128]{1,0:T(4,128)} %param.11) | copy-start | bytes 6148
  10.3 10.2 %collective-permute-start = (f32[6,1,4096]{2,0,1:T(8,128)S(1)}, f32[6,1,4096]{2,0,1:T(8,128)S(1)}, u32[]{:S(2)}, u32[]{:S(2)}) collective-permute-start(f32[6,1,4096]{2,0,1:T(8,128)S(1)} %get-tuple-element.40), channel_id=1, source_target_pairs={{1,0},{2,1},{3,2},{4,3},{5,4},{6,5},{7,6},{9,8},{10,9},{11,10},{12... | collective-permute-start | bytes 294920 | tf_op jit(solution)/shard_map/ppermute | solution.py:23
  11.6 10.1 %collective-permute-start.1 = (f32[6,1,4096]{2,0,1:T(8,128)S(1)}, f32[6,1,4096]{2,0,1:T(8,128)S(1)}, u32[]{:S(2)}, u32[]{:S(2)}) collective-permute-start(f32[6,1,4096]{2,0,1:T(8,128)S(1)} %get-tuple-element.41), channel_id=1, source_target_pairs={{0,1},{1,2},{2,3},{3,4},{4,5},{5,6},{6,7},{8,9},{9,10},{10,11},{11... | collective-permute-start | bytes 294920 | tf_op jit(solution)/shard_map/ppermute | solution.py:21
  24.7 8.1 %collective-permute-start.2 = (f32[6,1,4096]{2,0,1:T(8,128)S(1)}, f32[6,1,4096]{2,0,1:T(8,128)S(1)}, u32[]{:S(2)}, u32[]{:S(2)}) collective-permute-start(f32[6,1,4096]{2,0,1:T(8,128)S(1)} %get-tuple-element.30), channel_id=1, source_target_pairs={{1,0},{2,1},{3,2},{4,3},{5,4},{6,5},{7,6},{9,8},{10,9},{11,10},{12... | collective-permute-start | bytes 294920 | tf_op jit(solution)/shard_map/ppermute | solution.py:23
  26.0 9.7 %collective-permute-start.3 = (f32[6,1,4096]{2,0,1:T(8,128)S(1)}, f32[6,1,4096]{2,0,1:T(8,128)S(1)}, u32[]{:S(2)}, u32[]{:S(2)}) collective-permute-start(f32[6,1,4096]{2,0,1:T(8,128)S(1)} %get-tuple-element.31), channel_id=1, source_target_pairs={{0,1},{1,2},{2,3},{3,4},{4,5},{5,6},{6,7},{8,9},{9,10},{10,11},{11... | collective-permute-start | bytes 294920 | tf_op jit(solution)/shard_map/ppermute | solution.py:21
  36.5 8.1 %collective-permute-start.4 = (f32[6,1,4096]{2,0,1:T(8,128)S(1)}, f32[6,1,4096]{2,0,1:T(8,128)S(1)}, u32[]{:S(2)}, u32[]{:S(2)}) collective-permute-start(f32[6,1,4096]{2,0,1:T(8,128)S(1)} %get-tuple-element.28), channel_id=1, source_target_pairs={{1,0},{2,1},{3,2},{4,3},{5,4},{6,5},{7,6},{9,8},{10,9},{11,10},{12... | collective-permute-start | bytes 294920 | tf_op jit(solution)/shard_map/ppermute | solution.py:23
  37.8 9.7 %collective-permute-start.5 = (f32[6,1,4096]{2,0,1:T(8,128)S(1)}, f32[6,1,4096]{2,0,1:T(8,128)S(1)}, u32[]{:S(2)}, u32[]{:S(2)}) collective-permute-start(f32[6,1,4096]{2,0,1:T(8,128)S(1)} %get-tuple-element.29), channel_id=1, source_target_pairs={{0,1},{1,2},{2,3},{3,4},{4,5},{5,6},{6,7},{8,9},{9,10},{10,11},{11... | collective-permute-start | bytes 294920 | tf_op jit(solution)/shard_map/ppermute | solution.py:21
  50.5 22.9 %copy-start.3 = (f32[4,128]{1,0:T(4,128)S(1)}, f32[4,128]{1,0:T(4,128)}, u32[]{:S(2)}) copy-start(f32[4,128]{1,0:T(4,128)} %param.10) | copy-start | bytes 6148
  130.0 7.1 %collective-permute-start.6 = (f32[6,1,4096]{2,0,1:T(8,128)}, f32[6,1,4096]{2,0,1:T(8,128)S(1)}, u32[]{:S(2)}, u32[]{:S(2)}) collective-permute-start(f32[6,1,4096]{2,0,1:T(8,128)} %get-tuple-element.22), channel_id=1, source_target_pairs={{1,0},{2,1},{3,2},{4,3},{5,4},{6,5},{7,6},{9,8},{10,9},{11,10},{12... | collective-permute-start | bytes 294920 | tf_op jit(solution)/shard_map/ppermute | solution.py:23
  131.3 7.4 %collective-permute-start.7 = (f32[6,1,4096]{2,0,1:T(8,128)}, f32[6,1,4096]{2,0,1:T(8,128)S(1)}, u32[]{:S(2)}, u32[]{:S(2)}) collective-permute-start(f32[6,1,4096]{2,0,1:T(8,128)} %get-tuple-element.23), channel_id=1, source_target_pairs={{0,1},{1,2},{2,3},{3,4},{4,5},{5,6},{6,7},{8,9},{9,10},{10,11},{11... | collective-permute-start | bytes 294920 | tf_op jit(solution)/shard_map/ppermute | solution.py:21
Sparse Core Ops, SparseCore 0:
  158.1 77.1 reduce-scatter.1
where the time goes:
time: 243 us; the launch traced here: 242 us
  waiting for transfers between devices  88.8 us (37%)
  blocking collectives  53 us (22%)
  local copies, waits for them, and re-layouts  35.8 us (15%)
  starting transfers between devices  25.5 us (10%)
  other arithmetic  15.9 us (7%)
  between operations  14.3 us (6%)
  matrix products  8.79 us (4%)
    reduce_scatter x1, waiting for transfers between devices, body(): lax.psum_scatter(jnp.tensordot(own_rows, prior_model_outputs, axes=([0],...  77.3 us
    psum x1, blocking collectives, body(): gram_matrix, cross_term = lax.psum((gram_local, cross_local), 'band')  35.7 us
    ppermute x4, starting transfers between devices, with_halo(): lax.ppermute(tail, axis, [(i, (i + 1) % count) for i in range(ends)])  20.3 us
    dot_general x1, local copies, waits for them, and re-layouts, body(): jnp.tensordot(own_rows, prior_model_outputs, axes=([0], [0]), precision=l...  9.11 us
    reshape x1, local copies, waits for them, and re-layouts, body(): surface_height.reshape(local_members, -1)  8.99 us
    ppermute x4, waiting for transfers between devices, with_halo(): lax.ppermute(tail, axis, [(i, (i + 1) % count) for i in range(ends)])  8.62 us
    dot_general x1, matrix products, body(): jnp.tensordot(own_rows, prior_model_outputs, axes=([0], [0]), precision=l...  8.06 us
    psum x1, blocking collectives, body(): lax.psum(jnp.sum(modelled_water_levels, axis=0), 'mem')  6.87 us
  transfers between devices with their start and end apart: 9, of which 8 were waited for; matrix products, arithmetic and copies ran while one was open for 2% of the time, Pallas kernels for 0%

commit v1 on v0

--- a/solution.py
+++ b/solution.py
@@ -86,7 +86,9 @@
     centre = lax.psum(jnp.sum(modelled_water_levels, axis=0), "mem") / sample_trajectories
     spread_local = (modelled_water_levels - centre) / (obs_scale * norm_factor)
     spread, innovation_all = (
-        lax.all_gather(spread_local, "mem", axis=0, tiled=True),
+        jnp.concatenate(
+            lax.all_to_all(jnp.stack([spread_local] * lax.axis_size("mem")), "mem", 0, 0), axis=0
+        ),
         lax.all_gather(innovation, "mem", axis=0, tiled=True),
     )
     gram_local = jnp.dot(

time: 243 us -> 234 us (0.963)
  blocking collectives: 53 us -> 49 us
    ppermute x4, waiting for transfers between devices: 2.8 us -> 9.94 us  [with_halo(): lax.ppermute(head, axis, [((i + 1) % count, i) for i in range(ends)])]
    ppermute x4, waiting for transfers between devices: 8.62 us -> 2.53 us  [with_halo(): lax.ppermute(tail, axis, [(i, (i + 1) % count) for i in range(ends)])]
    all_gather x1 -> x0, blocking collectives: 5.23 us -> none  [body(): lax.all_gather(spread_local, 'mem', axis=0, tiled=True)]
    ppermute x4, starting transfers between devices: 20.3 us -> 17 us  [with_halo(): lax.ppermute(tail, axis, [(i, (i + 1) % count) for i in range(ends)])]
    all_to_all x0 -> x1, starting transfers between devices: none -> 3.28 us  [body(): lax.all_to_all(jnp.stack([spread_local] * lax.axis_size('mem')), 'mem', 0...]
    unnamed x15 -> x11, local copies, waits for them, and re-layouts: 3.03 us -> 0.03 us
    gather x1 -> x2, local copies, waits for them, and re-layouts: 6.8 us -> 6.91 us  [body(): jnp.take(surface_height.reshape(local_members, -1), local_cells, axis=1)]
  transfers between devices with their start and end apart: 9 -> 10, of which waited for: 8 -> 5; matrix products, arithmetic and copies ran while one was open for 2% -> 4% of each run, Pallas kernels for 0% -> 0%
where the time goes in v1:
time: 234 us; the launch traced here: 233 us
  waiting for transfers between devices  88.3 us (38%)
  blocking collectives  49 us (21%)
  local copies, waits for them, and re-layouts  33.8 us (14%)
  starting transfers between devices  25.5 us (11%)
  between operations  14.4 us (6%)
  other arithmetic  13.8 us (6%)
  matrix products  8.8 us (4%)
    reduce_scatter x1, waiting for transfers between devices, body(): lax.psum_scatter(jnp.tensordot(own_rows, prior_model_outputs, axes=([0],...  75.8 us
    psum x1, blocking collectives, body(): gram_matrix, cross_term = lax.psum((gram_local, cross_local), 'band')  38.1 us
    ppermute x4, starting transfers between devices, with_halo(): lax.ppermute(tail, axis, [(i, (i + 1) % count) for i in range(ends)])  17 us
    ppermute x4, waiting for transfers between devices, with_halo(): lax.ppermute(head, axis, [((i + 1) % count, i) for i in range(ends)])  9.94 us
    dot_general x1, local copies, waits for them, and re-layouts, body(): jnp.tensordot(own_rows, prior_model_outputs, axes=([0], [0]), precision=l...  9.34 us
    reshape x1, local copies, waits for them, and re-layouts, body(): surface_height.reshape(local_members, -1)  8.96 us
    dot_general x1, matrix products, body(): jnp.tensordot(own_rows, prior_model_outputs, axes=([0], [0]), precision=l...  8.06 us
    gather x2, local copies, waits for them, and re-layouts, body(): jnp.take(surface_height.reshape(local_members, -1), local_cells, axis=1)  6.91 us
  transfers between devices with their start and end apart: 10, of which 5 were waited for; matrix products, arithmetic and copies ran while one was open for 4% of the time, Pallas kernels for 0%

profile of v1, /device:TPU:0, one launch (start us, length us, event | category | flops | bytes accessed | tf_op | source)
XLA Modules:
  0.0 233.5 jit_solution(13909586901406182831)
XLA Ops:
  6.5 2.7 %fusion.57 = (f32[6,1,8,4096]{3,2,1,0:T(8,128)}, f32[6,1,8,4096]{3,2,1,0:T(8,128)S(1)}, f32[6,1,8,4096]{3,2,1,0:T(8,128)S(1)}) fusion(f32[6,3,8,4096]{3,2,1,0:T(8,128)} %param.7), kind=kLoop, calls=%fused_computation.92 | loop fusion | bytes 4718592 | tf_op jit(solution)/shard_map/slice | solution.py:52
  10.3 4.9 %collective-permute-start.1 = (f32[6,1,4096]{2,0,1:T(8,128)S(1)}, f32[6,1,4096]{2,0,1:T(8,128)S(1)}, u32[]{:S(2)}, u32[]{:S(2)}) collective-permute-start(f32[6,1,4096]{2,0,1:T(8,128)S(1)} %get-tuple-element.41), channel_id=1, source_target_pairs={{0,1},{1,2},{2,3},{3,4},{4,5},{5,6},{6,7},{8,9},{9,10},{10,11},{11... | collective-permute-start | bytes 294920 | tf_op jit(solution)/shard_map/ppermute | solution.py:21
  16.6 1.7 fusion.68
  19.0 3.0 %collective-permute-done = f32[6,1,4096]{2,0,1:T(8,128)S(1)} collective-permute-done((f32[6,1,4096]{2,0,1:T(8,128)S(1)}, f32[6,1,4096]{2,0,1:T(8,128)S(1)}, u32[]{:S(2)}, u32[]{:S(2)}) %collective-permute-start) | collective-permute-done | bytes 98336 | tf_op jit(solution)/shard_map/ppermute | solution.py:23
  22.1 2.6 %fusion.22 = f32[6,8,4096]{2,0,1:T(8,128)S(1)} fusion(f32[6,8,4096]{2,0,1:T(8,128)S(1)} %get-tuple-element.43, f32[6,1,4096]{2,0,1:T(8,128)S(1)} %collective-permute-done.1, f32[6,1,4096]{2,0,1:T(8,128)S(1)} %collective-permute-done, f32[6,8,1]{2,0,1:T(8,128)S(1)} %get-tuple-element.37, f32[6,8,4095]{2,0,1:T(8,128)} %get-tuple-element.39, ...), kind=kLoop, calls=%fused_computation.30 | loop fusion | flops 1769472 | bytes 4128768 | tf_op jit(solution)/shard_map/sub | solution.py:58
  25.1 4.3 %collective-permute-start.3 = (f32[6,1,4096]{2,0,1:T(8,128)S(1)}, f32[6,1,4096]{2,0,1:T(8,128)S(1)}, u32[]{:S(2)}, u32[]{:S(2)}) collective-permute-start(f32[6,1,4096]{2,0,1:T(8,128)S(1)} %get-tuple-element.31), channel_id=1, source_target_pairs={{0,1},{1,2},{2,3},{3,4},{4,5},{5,6},{6,7},{8,9},{9,10},{10,11},{11... | collective-permute-start | bytes 294920 | tf_op jit(solution)/shard_map/ppermute | solution.py:21
  32.4 3.9 %collective-permute-done.2 = f32[6,1,4096]{2,0,1:T(8,128)S(1)} collective-permute-done((f32[6,1,4096]{2,0,1:T(8,128)S(1)}, f32[6,1,4096]{2,0,1:T(8,128)S(1)}, u32[]{:S(2)}, u32[]{:S(2)}) %collective-permute-start.2) | collective-permute-done | bytes 98336 | tf_op jit(solution)/shard_map/ppermute | solution.py:23
  37.1 4.0 %collective-permute-start.5 = (f32[6,1,4096]{2,0,1:T(8,128)S(1)}, f32[6,1,4096]{2,0,1:T(8,128)S(1)}, u32[]{:S(2)}, u32[]{:S(2)}) collective-permute-start(f32[6,1,4096]{2,0,1:T(8,128)S(1)} %get-tuple-element.29), channel_id=1, source_target_pairs={{0,1},{1,2},{2,3},{3,4},{4,5},{5,6},{6,7},{8,9},{9,10},{10,11},{11... | collective-permute-start | bytes 294920 | tf_op jit(solution)/shard_map/ppermute | solution.py:21
  42.4 2.5 %collective-permute-done.5 = f32[6,1,4096]{2,0,1:T(8,128)S(1)} collective-permute-done((f32[6,1,4096]{2,0,1:T(8,128)S(1)}, f32[6,1,4096]{2,0,1:T(8,128)S(1)}, u32[]{:S(2)}, u32[]{:S(2)}) %collective-permute-start.5) | collective-permute-done | bytes 98336 | tf_op jit(solution)/shard_map/ppermute | solution.py:21
  45.0 3.0 %collective-permute-done.4 = f32[6,1,4096]{2,0,1:T(8,128)S(1)} collective-permute-done((f32[6,1,4096]{2,0,1:T(8,128)S(1)}, f32[6,1,4096]{2,0,1:T(8,128)S(1)}, u32[]{:S(2)}, u32[]{:S(2)}) %collective-permute-start.4) | collective-permute-done | bytes 98336 | tf_op jit(solution)/shard_map/ppermute | solution.py:23
  49.2 1.6 fusion.58
  50.8 9.0 %copy.36 = f32[6,32768]{0,1:T(8,128)} copy(f32[6,32768]{1,0:T(8,128)S(1)} %bitcast.84) | data formatting | bytes 1572864 | tf_op jit(solution)/shard_map/reshape | solution.py:77
  59.8 6.8 %gather_fusion = f32[512,6]{1,0:T(8,128)S(1)} fusion(f32[6,32768]{0,1:T(8,128)} %copy.36, s32[1024]{0:T(1024)S(1)} %pad_clamp_fusion), kind=kCustom, calls=%fused_computation | custom fusion | bytes 26624 | tf_op jit(solution)/shard_map/jit(_take)/gather | solution.py:77
  66.7 5.7 %psum.21 = f32[512]{0:T(512)S(1)} all-reduce(f32[512]{0:T(512)S(1)} %select_reduce_fusion), channel_id=1, replica_groups=mesh['mem'=4,'band'=8] {'mem'}, use_global_device_ids=true, to_apply=%region_1.2 | all-reduce | flops 512 | bytes 4096 | tf_op jit(solution)/shard_map/psum | solution.py:86
  73.0 3.3 %all-to-all-start = ((f32[4,6,512]{2,1,0:T(8,128)}), f32[4,6,512]{2,1,0:T(8,128)S(1)}, u32[]{:S(2)}, u32[]{:S(2)}) async-start(f32[4,6,512]{2,1,0:T(8,128)} %stack.19), calls=%async_computation | async-start | bytes 131072 | tf_op jit(solution)/shard_map/all_to_all | solution.py:90
  76.5 3.8 %collective-permute-start.7 = (f32[6,1,4096]{2,0,1:T(8,128)}, f32[6,1,4096]{2,0,1:T(8,128)S(1)}, u32[]{:S(2)}, u32[]{:S(2)}) collective-permute-start(f32[6,1,4096]{2,0,1:T(8,128)} %get-tuple-element.23), channel_id=1, source_target_pairs={{0,1},{1,2},{2,3},{3,4},{4,5},{5,6},{6,7},{8,9},{9,10},{10,11},{11... | collective-permute-start | bytes 294920 | tf_op jit(solution)/shard_map/ppermute | solution.py:21
  81.5 5.2 %all-gather = f32[4,6,512]{2,1,0:T(8,128)S(1)} all-gather(f32[1,6,512]{2,1,0:T(8,128)S(1)} %get-tuple-element.44), channel_id=1, replica_groups=mesh['mem'=4,'band'=8] {'mem'}, dimensions={0}, use_global_device_ids=true | all-gather | bytes 61440 | tf_op jit(solution)/shard_map/all_gather | solution.py:92
  87.2 38.1 %all-reduce = (f32[24,24]{1,0:T(8,128)S(1)}, f32[24,24]{1,0:T(8,128)S(1)}) all-reduce(f32[24,24]{1,0:T(8,128)S(1)} %fusion.72, f32[24,24]{1,0:T(8,128)S(1)} %fusion.71), channel_id=1, replica_groups=mesh['mem'=4,'band'=8] {'band'}, use_global_device_ids=true, to_apply=%region_5.6 | all-reduce | flops 1152 | bytes 9216 | tf_op jit(solution)/shard_map/psum | solution.py:103
  125.3 2.2 cholesky.13
  128.9 1.8 custom-call.8
  131.2 2.2 fusion.10
  133.4 8.1 %fusion = f32[24,3,8,4096]{3,0,2,1:T(8,128)S(1)} fusion(f32[6,1,8,4096]{3,0,2,1:T(8,128)S(1)} %get-tuple-element.9, f32[6,1,8,4096]{3,0,2,1:T(8,128)S(1)} %bitcast.86, f32[6,1,8,4096]{3,0,2,1:T(8,128)S(1)} %bitcast.85, f32[24,24]{1,0:T(8,128)S(1)} %get-tuple-element.49, s32[]{:T(128)S(6)} %select_n.33, pred[24,24]{1,0:T(8,128)(4,1)S(1)} %iota_compare_fusion.1, ...), kind=kOutput, calls=%fused_computation.1 | convolution fusion | flops 171049536 | bytes 12588548 | tf_op jit(solution)/shard_map/dot_general | solution.py:118
  141.5 9.3 %copy.39 = f32[24,3,8,4096]{3,2,1,0:T(8,128)} copy(f32[24,3,8,4096]{3,0,2,1:T(8,128)S(1)} %fusion) | data formatting | bytes 18874368 | tf_op jit(solution)/shard_map/dot_general | solution.py:118
  150.8 75.8 %reduce-scatter.2.cloned.1.call-done = f32[6,3,8,4096]{3,2,1,0:T(8,128)} async-done(((f32[24,3,8,4096]{3,2,1,0:T(8,128)}), f32[6,3,8,4096]{3,2,1,0:T(8,128)}) %reduce-scatter.2.cloned.1.call-update) | async-done | bytes 2359312 | tf_op jit(solution)/shard_map/reduce_scatter | solution.py:117
  (59 shorter events, 13.6 us)
Async XLA Ops:
  6.5 2.7 %copy-start = (f32[8,4096]{1,0:T(8,128)S(1)}, f32[8,4096]{1,0:T(8,128)}, u32[]{:S(2)}) copy-start(f32[8,4096]{1,0:T(8,128)} %param.8) | copy-start | bytes 393220
  10.2 8.0 %copy-start.4 = (s32[4,128]{1,0:T(4,128)S(1)}, s32[4,128]{1,0:T(4,128)}, u32[]{:S(2)}) copy-start(s32[4,128]{1,0:T(4,128)} %param.9) | copy-start | bytes 6148
  10.2 8.7 %copy-start.2 = (f32[4,128]{1,0:T(4,128)S(1)}, f32[4,128]{1,0:T(4,128)}, u32[]{:S(2)}) copy-start(f32[4,128]{1,0:T(4,128)} %param.11) | copy-start | bytes 6148
  10.3 8.7 %collective-permute-start.1 = (f32[6,1,4096]{2,0,1:T(8,128)S(1)}, f32[6,1,4096]{2,0,1:T(8,128)S(1)}, u32[]{:S(2)}, u32[]{:S(2)}) collective-permute-start(f32[6,1,4096]{2,0,1:T(8,128)S(1)} %get-tuple-element.41), channel_id=1, source_target_pairs={{0,1},{1,2},{2,3},{3,4},{4,5},{5,6},{6,7},{8,9},{9,10},{10,11},{11... | collective-permute-start | bytes 294920 | tf_op jit(solution)/shard_map/ppermute | solution.py:21
  15.2 6.9 %collective-permute-start = (f32[6,1,4096]{2,0,1:T(8,128)S(1)}, f32[6,1,4096]{2,0,1:T(8,128)S(1)}, u32[]{:S(2)}, u32[]{:S(2)}) collective-permute-start(f32[6,1,4096]{2,0,1:T(8,128)S(1)} %get-tuple-element.40), channel_id=1, source_target_pairs={{1,0},{2,1},{3,2},{4,3},{5,4},{6,5},{7,6},{9,8},{10,9},{11,10},{12... | collective-permute-start | bytes 294920 | tf_op jit(solution)/shard_map/ppermute | solution.py:23
  25.1 7.2 %collective-permute-start.3 = (f32[6,1,4096]{2,0,1:T(8,128)S(1)}, f32[6,1,4096]{2,0,1:T(8,128)S(1)}, u32[]{:S(2)}, u32[]{:S(2)}) collective-permute-start(f32[6,1,4096]{2,0,1:T(8,128)S(1)} %get-tuple-element.31), channel_id=1, source_target_pairs={{0,1},{1,2},{2,3},{3,4},{4,5},{5,6},{6,7},{8,9},{9,10},{10,11},{11... | collective-permute-start | bytes 294920 | tf_op jit(solution)/shard_map/ppermute | solution.py:21
  29.5 6.9 %collective-permute-start.2 = (f32[6,1,4096]{2,0,1:T(8,128)S(1)}, f32[6,1,4096]{2,0,1:T(8,128)S(1)}, u32[]{:S(2)}, u32[]{:S(2)}) collective-permute-start(f32[6,1,4096]{2,0,1:T(8,128)S(1)} %get-tuple-element.30), channel_id=1, source_target_pairs={{1,0},{2,1},{3,2},{4,3},{5,4},{6,5},{7,6},{9,8},{10,9},{11,10},{12... | collective-permute-start | bytes 294920 | tf_op jit(solution)/shard_map/ppermute | solution.py:23
  37.1 7.9 %collective-permute-start.5 = (f32[6,1,4096]{2,0,1:T(8,128)S(1)}, f32[6,1,4096]{2,0,1:T(8,128)S(1)}, u32[]{:S(2)}, u32[]{:S(2)}) collective-permute-start(f32[6,1,4096]{2,0,1:T(8,128)S(1)} %get-tuple-element.29), channel_id=1, source_target_pairs={{0,1},{1,2},{2,3},{3,4},{4,5},{5,6},{6,7},{8,9},{9,10},{10,11},{11... | collective-permute-start | bytes 294920 | tf_op jit(solution)/shard_map/ppermute | solution.py:21
  41.1 6.9 %collective-permute-start.4 = (f32[6,1,4096]{2,0,1:T(8,128)S(1)}, f32[6,1,4096]{2,0,1:T(8,128)S(1)}, u32[]{:S(2)}, u32[]{:S(2)}) collective-permute-start(f32[6,1,4096]{2,0,1:T(8,128)S(1)} %get-tuple-element.28), channel_id=1, source_target_pairs={{1,0},{2,1},{3,2},{4,3},{5,4},{6,5},{7,6},{9,8},{10,9},{11,10},{12... | collective-permute-start | bytes 294920 | tf_op jit(solution)/shard_map/ppermute | solution.py:23
  50.8 21.6 %copy-start.1 = (f32[6,4,128]{2,1,0:T(4,128)S(1)}, f32[6,4,128]{2,1,0:T(4,128)}, u32[]{:S(2)}) copy-start(f32[6,4,128]{2,1,0:T(4,128)} %param.12) | copy-start | bytes 36868
  50.8 21.6 %copy-start.3 = (f32[4,128]{1,0:T(4,128)S(1)}, f32[4,128]{1,0:T(4,128)}, u32[]{:S(2)}) copy-start(f32[4,128]{1,0:T(4,128)} %param.10) | copy-start | bytes 6148
  73.0 13.7 %all-to-all-start = ((f32[4,6,512]{2,1,0:T(8,128)}), f32[4,6,512]{2,1,0:T(8,128)S(1)}, u32[]{:S(2)}, u32[]{:S(2)}) async-start(f32[4,6,512]{2,1,0:T(8,128)} %stack.19), calls=%async_computation | async-start | bytes 131072 | tf_op jit(solution)/shard_map/all_to_all | solution.py:90
  76.3 150.3 %reduce-scatter.2.cloned.1.call-start = ((), (), s32[]{:S(2)}) async-start(), calls=%async_computation.2 | async-start | bytes 11796480 | tf_op jit(solution)/shard_map/reduce_scatter | solution.py:117
  76.5 54.7 %collective-permute-start.7 = (f32[6,1,4096]{2,0,1:T(8,128)}, f32[6,1,4096]{2,0,1:T(8,128)S(1)}, u32[]{:S(2)}, u32[]{:S(2)}) collective-permute-start(f32[6,1,4096]{2,0,1:T(8,128)} %get-tuple-element.23), channel_id=1, source_target_pairs={{0,1},{1,2},{2,3},{3,4},{4,5},{5,6},{6,7},{8,9},{9,10},{10,11},{11... | collective-permute-start | bytes 294920 | tf_op jit(solution)/shard_map/ppermute | solution.py:21
  80.2 50.9 %collective-permute-start.6 = (f32[6,1,4096]{2,0,1:T(8,128)}, f32[6,1,4096]{2,0,1:T(8,128)}, u32[]{:S(2)}, u32[]{:S(2)}) collective-permute-start(f32[6,1,4096]{2,0,1:T(8,128)} %get-tuple-element.22), channel_id=1, source_target_pairs={{1,0},{2,1},{3,2},{4,3},{5,4},{6,5},{7,6},{9,8},{10,9},{11,10},{12... | collective-permute-start | bytes 294920 | tf_op jit(solution)/shard_map/ppermute | solution.py:23
Sparse Core Ops, SparseCore 0:
  151.0 75.6 reduce-scatter.1
